TPU v7x, 32 devices: a whole 2x2x4 slice. The times are simulated.
32 devices in a mesh: dp: 2 (over x), ctx: 4 (over y, core), tp: 4 (over z).
Axes of the slice: x: 2, y: 2, z: 4, core: 2. Of those that a mesh axis runs over, the one named last changes fastest.
Arguments:
- tokens: bfloat16 [16384, 768], P(('dp', 'ctx', 'tp')), may hold values from -6 to 6
- first_gain: bfloat16 [768], replicated, may hold values from 0.5 to 1.5
- first_bias: bfloat16 [768], replicated, may hold values from -0.4375 to 0.4375
- mixer_weight: bfloat16 [768, 3, 768], P(None, None, 'tp'), may hold values from -0.21875 to 0.21875
- mixer_bias: bfloat16 [3, 768], P(None, 'tp'), may hold values from -0.3125 to 0.3125
- feature_weight: bfloat16 [2, 12, 64, 64], P(None, 'tp'), may hold values from -1.5 to 1.5
- feature_bias: bfloat16 [2, 12, 64], P(None, 'tp'), may hold values from -6 to 6
- output_weight: bfloat16 [768, 768], P('tp'), may hold values from -6 to 6
- output_bias: bfloat16 [768], replicated, may hold values from -4 to 4
- second_gain: bfloat16 [768], replicated, may hold values from 0.5 to 1.5
- second_bias: bfloat16 [768], replicated, may hold values from -4 to 4
- inner_weight: bfloat16 [768, 3072], P(None, 'tp'), may hold values from -0.21875 to 0.21875
- inner_bias: bfloat16 [3072], P('tp'), may hold values from -4 to 4
- outer_weight: bfloat16 [3072, 768], P('tp'), may hold values from -0.109375 to 0.109375
- outer_bias: bfloat16 [768], replicated, may hold values from -4 to 4
- block_owner: int32 [2, 32], P('dp'), may hold values from 0 to 0, as said below
- cotangent: bfloat16 [16384, 768], P(('dp', 'ctx', 'tp')), may hold values from -6 to 6
Outputs:
- result: bfloat16 [16384, 768], P(('dp', 'ctx', 'tp'))
- tokens_gradient: float32 [16384, 768], P(('dp', 'ctx', 'tp'))
- first_gain_gradient: float32 [768], replicated
- first_bias_gradient: float32 [768], replicated
- mixer_weight_gradient: float32 [768, 3, 768], P(None, None, 'tp')
- mixer_bias_gradient: float32 [3, 768], P(None, 'tp')
- feature_weight_gradient: float32 [2, 12, 64, 64], P(None, 'tp')
- feature_bias_gradient: float32 [2, 12, 64], P(None, 'tp')
- output_weight_gradient: float32 [768, 768], P('tp')
- output_bias_gradient: float32 [768], replicated
- second_gain_gradient: float32 [768], replicated
- second_bias_gradient: float32 [768], replicated
- inner_weight_gradient: float32 [768, 3072], P(None, 'tp')
- inner_bias_gradient: float32 [3072], P('tp')
- outer_weight_gradient: float32 [3072, 768], P('tp')
- outer_bias_gradient: float32 [768], replicated
Inputs may be any that keep to these rules, and one draw needn't show every extreme that they name: `block_owner`: all blocks of one sequence carry one number, and pieces of a data group share the same blocks. A sequence covers 8192 // 256 or twice that many consecutive blocks of every piece, so it has 8192 or 16384 tokens; its number is the index of its last 8192-token unit, so numbers rise along a row, differ between sequences, and the last block of every row carries 1 - 1.
All inputs are finite; a program needn't handle non-finite values.
Results may differ from a plain program's by a relative error of at most 0.015.
Values may be sent and summed in bfloat16 or wider, within the bound.
A program may use at most 128 MiB of HBM per device.

v0:
```python
import jax
import jax.numpy as jnp
from jax import lax
from jax.sharding import PartitionSpec as P

HD = 64
BLOCK = 64
SHORT = 8192
EPSILON = 1e-05
HIGHEST = lax.Precision.HIGHEST


def entering(x, axis, combine, identity, reverse):
    peers, mine = (lax.axis_size(axis), lax.axis_index(axis))
    everything = jax.tree.map(lambda part: lax.all_gather(part, axis), x)
    start = jax.tree.map(
        lambda part, zero: jnp.broadcast_to(jnp.asarray(zero, part.dtype), part.shape), x, identity
    )

    def turn(k, before):
        at = peers - 1 - k if reverse else k
        reached = at > mine if reverse else at < mine
        new = combine(before, jax.tree.map(lambda part: part[at], everything))
        return jax.tree.map(lambda a, b: jnp.where(reached, a, b), new, before)

    return lax.fori_loop(0, peers, turn, start)


def layer_norm(values, norm_gain, norm_offset):
    average = jnp.mean(values, axis=-1, keepdims=True)
    centered = values - average
    variance = jnp.mean(centered * centered, axis=-1, keepdims=True)
    return centered * lax.rsqrt(variance + EPSILON) * norm_gain + norm_offset


def gaussian_unit(values):
    return (
        0.5
        * values
        * (1.0 + jnp.tanh(0.7978845608028654 * (values + 0.044715 * values * values * values)))
    )


def feature_map(inputs, weight, offset):
    logits = jnp.einsum("thd,hde->the", inputs, weight, precision=HIGHEST) + offset
    return jnp.concatenate(
        [jax.nn.softmax(logits, axis=-1), jax.nn.softmax(-logits, axis=-1)], axis=-1
    )


def rounded(values):
    return lax.optimization_barrier(values.astype(jnp.bfloat16)).astype(jnp.float32)


def add_pair(first_pair, second_pair):
    return (first_pair[0] + second_pair[0], first_pair[1] + second_pair[1])


def shards(
    tokens,
    first_gain,
    first_bias,
    mixer_weight,
    mixer_bias,
    feature_weight,
    feature_bias,
    output_weight,
    output_bias,
    second_gain,
    second_bias,
    inner_weight,
    inner_bias,
    outer_weight,
    outer_bias,
    block_owner,
    cotangent,
):
    local_rows, model_width = tokens.shape
    heads_here = mixer_weight.shape[2] // HD
    piece_rows = local_rows * lax.axis_size("tp")
    blocks = piece_rows // BLOCK
    unit_count = piece_rows * lax.axis_size("ctx") // SHORT
    owners = block_owner[0]
    block_index = jnp.arange(blocks)
    member = (owners[:, None] == jnp.arange(unit_count)[None, :]).astype(jnp.float32)
    earlier = (
        (owners[:, None] == owners[None, :]) & (block_index[:, None] > block_index[None, :])
    ).astype(jnp.float32)
    causal = jnp.arange(BLOCK)[:, None] >= jnp.arange(BLOCK)[None, :]
    inputs = tokens.astype(jnp.float32)
    first_normed, first_pull = jax.vjp(
        layer_norm, inputs, first_gain.astype(jnp.float32), first_bias.astype(jnp.float32)
    )
    first_low = first_normed.astype(jnp.bfloat16)
    first_rows = lax.all_gather(first_low, "tp", axis=0, tiled=True)
    mixer_flat = mixer_weight.reshape(model_width, -1)
    mixed_rows = jnp.dot(
        first_rows, mixer_flat, preferred_element_type=jnp.float32
    ) + mixer_bias.astype(jnp.float32).reshape(-1)
    mixed_low = mixed_rows.astype(jnp.bfloat16).reshape(piece_rows, 3, heads_here, HD)
    query_rows = mixed_low[:, 0]
    key_rows = mixed_low[:, 1]
    value_rows = mixed_low[:, 2]
    weight_float = feature_weight.astype(jnp.float32)
    bias_float = feature_bias.astype(jnp.float32)
    query_lifted, query_pull = jax.vjp(
        feature_map, query_rows.astype(jnp.float32), weight_float[0], bias_float[0]
    )
    key_lifted, key_pull = jax.vjp(
        feature_map, key_rows.astype(jnp.float32), weight_float[1], bias_float[1]
    )
    query_blocks = query_lifted.astype(jnp.bfloat16).reshape(blocks, BLOCK, heads_here, 2 * HD)
    key_blocks = key_lifted.astype(jnp.bfloat16).reshape(blocks, BLOCK, heads_here, 2 * HD)
    value_blocks = value_rows.reshape(blocks, BLOCK, heads_here, HD)
    block_state = jnp.einsum(
        "jthe,jthf->jhef", value_blocks, key_blocks, preferred_element_type=jnp.float32
    )
    block_norm = jnp.sum(key_blocks.astype(jnp.float32), axis=1)
    totals = (
        jnp.einsum("js,jhef->shef", member, block_state, precision=HIGHEST),
        jnp.einsum("js,jhf->shf", member, block_norm, precision=HIGHEST),
    )
    incoming = entering(
        (totals[0], totals[1]),
        "ctx",
        add_pair,
        (jnp.zeros_like(totals[0]), jnp.zeros_like(totals[1])),
        False,
    )
    state_before = jnp.einsum(
        "ji,ihef->jhef", earlier, block_state, precision=HIGHEST
    ) + jnp.einsum("js,shef->jhef", member, incoming[0], precision=HIGHEST)
    norm_before = jnp.einsum("ji,ihf->jhf", earlier, block_norm, precision=HIGHEST) + jnp.einsum(
        "js,shf->jhf", member, incoming[1], precision=HIGHEST
    )
    numerator = jnp.einsum(
        "jthf,jhef->jthe",
        query_blocks,
        state_before,
        precision=HIGHEST,
        preferred_element_type=jnp.float32,
    )
    denominator = jnp.einsum(
        "jthf,jhf->jth",
        query_blocks,
        norm_before,
        precision=HIGHEST,
        preferred_element_type=jnp.float32,
    )
    scores = jnp.einsum(
        "jthf,jshf->jhts", query_blocks, key_blocks, preferred_element_type=jnp.float32
    )
    scores_low = jnp.where(causal, scores, 0.0).astype(jnp.bfloat16)
    numerator = numerator + jnp.einsum(
        "jhts,jshe->jthe", scores_low, value_blocks, preferred_element_type=jnp.float32
    )
    denominator = denominator + jnp.swapaxes(jnp.sum(scores_low.astype(jnp.float32), axis=-1), 1, 2)
    attended = numerator / denominator[..., None]
    attended_low = attended.astype(jnp.bfloat16).reshape(piece_rows, heads_here * HD)
    attention_sum = lax.psum_scatter(
        jnp.dot(attended_low, output_weight, preferred_element_type=jnp.float32),
        "tp",
        scatter_dimension=0,
        tiled=True,
    )
    middle = inputs + attention_sum + output_bias.astype(jnp.float32)
    second_normed, second_pull = jax.vjp(
        layer_norm, middle, second_gain.astype(jnp.float32), second_bias.astype(jnp.float32)
    )
    second_low = second_normed.astype(jnp.bfloat16)
    second_rows = lax.all_gather(second_low, "tp", axis=0, tiled=True)
    hidden_input = jnp.dot(
        second_rows, inner_weight, preferred_element_type=jnp.float32
    ) + inner_bias.astype(jnp.float32)
    activated_float, curve_pull = jax.vjp(gaussian_unit, hidden_input)
    activated = activated_float.astype(jnp.bfloat16)
    branch_out = lax.psum_scatter(
        jnp.dot(activated, outer_weight, preferred_element_type=jnp.float32).astype(jnp.bfloat16),
        "tp",
        scatter_dimension=0,
        tiled=True,
    ).astype(jnp.float32)
    result = (middle + branch_out + outer_bias.astype(jnp.float32)).astype(jnp.bfloat16)
    upstream = cotangent.astype(jnp.float32)
    upstream_rows = lax.all_gather(cotangent, "tp", axis=0, tiled=True)
    outer_delta = jnp.einsum(
        "tf,td->fd", activated, upstream_rows, preferred_element_type=jnp.float32
    )
    activated_delta = jnp.einsum(
        "td,fd->tf", upstream_rows, outer_weight, preferred_element_type=jnp.float32
    )
    (hidden_delta,) = curve_pull(activated_delta)
    hidden_low = hidden_delta.astype(jnp.bfloat16)
    inner_bias_delta = jnp.sum(hidden_low.astype(jnp.float32), axis=0)
    inner_delta = jnp.einsum(
        "td,tf->df", second_rows, hidden_low, preferred_element_type=jnp.float32
    )
    second_delta = lax.psum_scatter(
        jnp.einsum("tf,df->td", hidden_low, inner_weight, preferred_element_type=jnp.float32),
        "tp",
        scatter_dimension=0,
        tiled=True,
    )
    middle_back, second_gain_part, second_bias_part = second_pull(second_delta)
    middle_delta = upstream + middle_back
    middle_low = middle_delta.astype(jnp.bfloat16)
    middle_rows = lax.all_gather(middle_low, "tp", axis=0, tiled=True)
    output_delta = jnp.einsum(
        "tk,td->kd", attended_low, middle_rows, preferred_element_type=jnp.float32
    )
    attended_delta = rounded(
        jnp.einsum("td,kd->tk", middle_rows, output_weight, preferred_element_type=jnp.float32)
    )
    attended_delta = attended_delta.reshape(blocks, BLOCK, heads_here, HD)
    numerator_delta = attended_delta / denominator[..., None]
    denominator_delta = -jnp.sum(attended_delta * attended, axis=-1) / denominator
    score_delta = (
        jnp.einsum(
            "jthe,jshe->jhts",
            numerator_delta,
            value_blocks,
            precision=HIGHEST,
            preferred_element_type=jnp.float32,
        )
        + jnp.swapaxes(denominator_delta, 1, 2)[..., None]
    )
    score_low = jnp.where(causal, score_delta, 0.0).astype(jnp.bfloat16)
    value_delta = jnp.einsum(
        "jhts,jthe->jshe",
        scores_low,
        numerator_delta,
        precision=HIGHEST,
        preferred_element_type=jnp.float32,
    )
    query_delta = (
        jnp.einsum("jhts,jshf->jthf", score_low, key_blocks, preferred_element_type=jnp.float32)
        + jnp.einsum(
            "jthe,jhef->jthf",
            numerator_delta,
            state_before,
            precision=HIGHEST,
            preferred_element_type=jnp.float32,
        )
        + denominator_delta[..., None] * norm_before[:, None]
    )
    key_delta = jnp.einsum(
        "jhts,jthf->jshf", score_low, query_blocks, preferred_element_type=jnp.float32
    )
    before_delta = jnp.einsum(
        "jthf,jthe->jhef",
        query_blocks,
        numerator_delta,
        precision=HIGHEST,
        preferred_element_type=jnp.float32,
    )
    norm_before_delta = jnp.einsum(
        "jthf,jth->jhf",
        query_blocks,
        denominator_delta,
        precision=HIGHEST,
        preferred_element_type=jnp.float32,
    )
    leaving = (
        jnp.einsum("js,jhef->shef", member, before_delta, precision=HIGHEST),
        jnp.einsum("js,jhf->shf", member, norm_before_delta, precision=HIGHEST),
    )
    later_sums = entering(
        (leaving[0], leaving[1]),
        "ctx",
        add_pair,
        (jnp.zeros_like(leaving[0]), jnp.zeros_like(leaving[1])),
        True,
    )
    state_delta = jnp.einsum(
        "ji,jhef->ihef", earlier, before_delta, precision=HIGHEST
    ) + jnp.einsum("js,shef->jhef", member, later_sums[0], precision=HIGHEST)
    block_norm_delta = jnp.einsum(
        "ji,jhf->ihf", earlier, norm_before_delta, precision=HIGHEST
    ) + jnp.einsum("js,shf->jhf", member, later_sums[1], precision=HIGHEST)
    value_delta = value_delta + jnp.einsum(
        "jhef,jthf->jthe",
        state_delta,
        key_blocks,
        precision=HIGHEST,
        preferred_element_type=jnp.float32,
    )
    key_delta = (
        key_delta
        + jnp.einsum(
            "jhef,jthe->jthf",
            state_delta,
            value_blocks,
            precision=HIGHEST,
            preferred_element_type=jnp.float32,
        )
        + block_norm_delta[:, None]
    )
    query_in_delta, query_weight_delta, query_bias_delta = query_pull(
        rounded(query_delta).reshape(piece_rows, heads_here, 2 * HD)
    )
    key_in_delta, key_weight_delta, key_bias_delta = key_pull(
        rounded(key_delta).reshape(piece_rows, heads_here, 2 * HD)
    )
    mixed_delta = jnp.stack(
        [query_in_delta, key_in_delta, value_delta.reshape(piece_rows, heads_here, HD)], axis=1
    )
    mixed_delta = mixed_delta.astype(jnp.bfloat16).reshape(piece_rows, 3 * heads_here * HD)
    mixer_bias_delta = jnp.sum(mixed_delta.astype(jnp.float32), axis=0).reshape(3, heads_here * HD)
    mixer_delta = jnp.einsum(
        "td,tk->dk", first_rows, mixed_delta, preferred_element_type=jnp.float32
    ).reshape(model_width, 3, heads_here * HD)
    first_delta = lax.psum_scatter(
        jnp.einsum("tk,dk->td", mixed_delta, mixer_flat, preferred_element_type=jnp.float32).astype(
            jnp.bfloat16
        ),
        "tp",
        scatter_dimension=0,
        tiled=True,
    ).astype(jnp.float32)
    input_back, first_gain_part, first_bias_part = first_pull(first_delta)
    tokens_delta = middle_delta + input_back
    feature_weight_delta = jnp.stack([query_weight_delta, key_weight_delta])
    feature_bias_delta = jnp.stack([query_bias_delta, key_bias_delta])
    output_bias_part = jnp.sum(middle_delta, axis=0)
    outer_bias_part = jnp.sum(upstream, axis=0)
    summed = lax.psum(
        (
            mixer_delta,
            mixer_bias_delta,
            feature_weight_delta,
            feature_bias_delta,
            output_delta,
            inner_delta,
            inner_bias_delta,
            outer_delta,
            first_gain_part,
            first_bias_part,
            output_bias_part,
            second_gain_part,
            second_bias_part,
            outer_bias_part,
        ),
        ("dp", "ctx"),
    )
    shared = lax.psum((summed[8], summed[9], summed[10], summed[11], summed[12], summed[13]), "tp")
    return (
        result,
        tokens_delta,
        shared[0],
        shared[1],
        summed[0],
        summed[1],
        summed[2],
        summed[3],
        summed[4],
        shared[2],
        shared[3],
        shared[4],
        summed[5],
        summed[6],
        summed[7],
        shared[5],
    )


def solution(mesh):
    in_specs = (
        P(("dp", "ctx", "tp"), None),
        P(),
        P(),
        P(None, None, "tp"),
        P(None, "tp"),
        P(None, "tp", None, None),
        P(None, "tp", None),
        P("tp", None),
        P(),
        P(),
        P(),
        P(None, "tp"),
        P("tp"),
        P("tp", None),
        P(),
        P("dp", None),
        P(("dp", "ctx", "tp"), None),
    )
    out_specs = (
        P(("dp", "ctx", "tp"), None),
        P(("dp", "ctx", "tp"), None),
        P(),
        P(),
        P(None, None, "tp"),
        P(None, "tp"),
        P(None, "tp", None, None),
        P(None, "tp", None),
        P("tp", None),
        P(),
        P(),
        P(),
        P(None, "tp"),
        P("tp"),
        P("tp", None),
        P(),
    )
    return jax.shard_map(shards, mesh=mesh, in_specs=in_specs, out_specs=out_specs, check_vma=False)
```

profile of v0, /device:TPU:0, one launch (start us, length us, event | category | flops | bytes accessed | tf_op | source)
XLA Modules:
  0.0 1006.3 jit_solution(10132067115701984201)
XLA Ops:
  14.2 65.0 %all-gather.11.cloned.1.call-done = bf16[2048,768]{1,0:T(8,128)(2,1)} async-done(((bf16[512,768]{1,0:T(8,128)(2,1)}), bf16[2048,768]{1,0:T(8,128)(2,1)}) %all-gather.11.cloned.1.call-update) | async-done | bytes 3145744 | tf_op jit(solution)/shard_map/all_gather | solution.py:95
  79.2 3.9 add_convert_fusion
  94.4 3.4 reshape_squeeze.3
  97.8 3.4 copy.124
  103.5 3.4 concatenate.19
  117.1 4.3 convert_reduce_fusion.3
  121.6 5.6 all-gather.4
  129.9 3.5 copy.115
  135.1 3.4 concatenate.21
  138.5 3.5 copy.114
  147.0 7.0 all-gather
  154.0 6.5 while.34
  161.7 5.7 multiply_add_fusion.3
  171.9 4.7 fusion.25
  184.6 3.7 fusion.127
  189.6 108.3 %reduce-scatter.5.cloned.1.call-done = f32[512,768]{1,0:T(8,128)} async-done(((f32[2048,768]{1,0:T(8,128)}), f32[512,768]{1,0:T(8,128)}) %reduce-scatter.5.cloned.1.call-update) | async-done | bytes 1572880 | tf_op jit(solution)/shard_map/reduce_scatter | solution.py:160
  303.6 62.3 %all-gather.13.cloned.1.call-done = bf16[2048,768]{1,0:T(8,128)(2,1)} async-done(((bf16[512,768]{1,0:T(8,128)(2,1)}), bf16[2048,768]{1,0:T(8,128)(2,1)}) %all-gather.13.cloned.1.call-update) | async-done | bytes 3145744 | tf_op jit(solution)/shard_map/all_gather | solution.py:171
  365.9 7.5 fusion.128
  373.4 56.1 %all-gather.15.cloned.1.call-done = bf16[2048,768]{1,0:T(8,128)(2,1)} async-done(((bf16[512,768]{1,0:T(8,128)(2,1)}), bf16[2048,768]{1,0:T(8,128)(2,1)}) %all-gather.15.cloned.1.call-update) | async-done | bytes 3145744 | tf_op jit(solution)/shard_map/all_gather | solution.py:185
  429.5 12.2 %convert_reduce_fusion = (f32[768]{0:T(1024)}, bf16[2048,768]{1,0:T(8,128)(2,1)S(1)}, bf16[2048,768]{1,0:T(8,128)(2,1)}) fusion(f32[2048,768]{1,0:T(8,128)} %fusion.128, f32[768]{0:T(1024)} %convert_element_type.136, bf16[2048,768]{1,0:T(8,128)(2,1)} %all-gather.15.cloned.1.call-done, bf16[768,768]{1,0:T(8,128)(2,1)S(1)} %copy-done), kind=kOutput, calls=%fused_computation.18 | convolution fusion | flops 2461531392 | bytes 16914432 | tf_op jit(solution)/shard_map/td,fd->tf/dot_general | solution.py:189
  443.4 4.6 fusion.129
  448.1 6.3 convolution_convert_fusion
  455.0 102.6 %reduce-scatter.9.cloned.1.call-done = f32[512,768]{1,0:T(8,128)} async-done(((f32[2048,768]{1,0:T(8,128)}), f32[512,768]{1,0:T(8,128)}) %reduce-scatter.9.cloned.1.call-update) | async-done | bytes 1572880 | tf_op jit(solution)/shard_map/reduce_scatter | solution.py:198
  560.2 60.3 %reduce-scatter.7.cloned.1.call-done = bf16[512,768]{1,0:T(8,128)(2,1)} async-done(((bf16[2048,768]{1,0:T(8,128)(2,1)}), bf16[512,768]{1,0:T(8,128)(2,1)}) %reduce-scatter.7.cloned.1.call-update) | async-done | bytes 786448 | tf_op jit(solution)/shard_map/reduce_scatter | solution.py:177
  629.5 60.4 %all-gather.17.cloned.1.call-done = bf16[2048,768]{1,0:T(8,128)(2,1)} async-done(((bf16[512,768]{1,0:T(8,128)(2,1)}), bf16[2048,768]{1,0:T(8,128)(2,1)}) %all-gather.17.cloned.1.call-update) | async-done | bytes 3145744 | tf_op jit(solution)/shard_map/all_gather | solution.py:207
  695.6 5.2 multiply_reduce_fusion
  701.0 10.8 %fusion.23 = f32[32,3,128,64]{2,3,1,0:T(8,128)} fusion(f32[32,3,64,128]{3,0,2,1:T(8,128)S(1)} %copy-done.27, f32[32,64,3,64]{1,0,3,2:T(8,128)S(1)} %copy-done.24, f32[32,64,3]{1,2,0:T(4,128)S(1)} %copy-done.56), kind=kOutput, calls=%fused_computation.50 | convolution fusion | flops 604372992 | bytes 7888896 | tf_op jit(solution)/shard_map/jthe,jhef->jthf/dot_general | solution.py:237
  711.8 4.3 fusion.111
  717.6 5.2 all-gather.5
  725.7 6.5 all-gather.2
  733.0 5.7 multiply_add_fusion.2
  738.7 4.8 fusion.15
  743.6 4.5 fusion.17
  748.1 4.4 select_convert_fusion
  756.5 4.9 bitcast_add_fusion
  767.2 3.7 fusion.119
  770.9 3.4 copy.180
  776.1 3.4 copy.181
  781.8 3.6 fusion.118
  790.9 3.6 copy.179
  797.4 4.9 fusion.113
  806.1 4.1 convolution_convert_fusion.1
  810.5 7.0 fusion.132
  817.5 4.1 fusion.131
  830.0 39.3 %reduce-scatter.11.cloned.1.call-done = bf16[512,768]{1,0:T(8,128)(2,1)} async-done(((bf16[2048,768]{1,0:T(8,128)(2,1)}), bf16[512,768]{1,0:T(8,128)(2,1)}) %reduce-scatter.11.cloned.1.call-update) | async-done | bytes 786448 | tf_op jit(solution)/shard_map/reduce_scatter | solution.py:312
  875.3 26.5 %all-reduce = (f32[768]{0:T(1024)S(1)}, f32[768]{0:T(1024)S(1)}, f32[3,192]{1,0:T(4,128)}, f32[2,3,64]{2,1,0:T(4,128)S(1)}, f32[768]{0:T(1024)S(1)}, /*index=5*/...) all-reduce(f32[768]{0:T(1024)S(1)} %get-tuple-element.373, ...), channel_id=1, replica_groups=mesh['dp'=2,'ctx'=4,'tp'=4] {'dp','ctx'}, use_global_device_ids=true, to_apply=%region_32.33 | all-reduce | flops 6336 | bytes 50688 | tf_op jit(solution)/shard_map/psum | solution.py:326
  902.4 18.5 %all-reduce.2 = (f32[768]{0:T(1024)}, f32[768]{0:T(1024)}, f32[768]{0:T(1024)}, f32[768]{0:T(1024)}, f32[768]{0:T(1024)}, /*index=5*/f32[768]{0:T(1024)}) all-reduce(f32[768]{0:T(1024)S(1)} %get-tuple-element.404, f32[768]{0:T(1024)S(1)} %get-tuple-element.405, ...), channel_id=1, replica_groups=mesh['dp'=2,'ctx'=4,'tp'=4] {'tp'}, use_global_device_ids=true, to_apply=%region_33.34 | all-reduce | flops 4608 | bytes 36864 | tf_op jit(solution)/shard_map/psum | solution.py:345
  920.9 70.3 %all-reduce.5.cloned.1.call-done = (f32[768,3,192]{0,2,1:T(8,128)}, f32[2,3,64,64]{3,2,1,0:T(8,128)}, f32[192,768]{1,0:T(8,128)}, f32[768,768]{1,0:T(8,128)}, f32[768,768]{1,0:T(8,128)}) async-done(((f32[768,3,192]{0,2,1:T(8,128)}, f32[2,3,64,64]{3,2,1,0:T(8,128)}, f32[192,768]{1,0:T(8,128)}, f32[768,768]{1,0:T(8,128)}, f32[768,768]{1,0:T(8,128)}), (f32[768,3,192]{0,2,1:T(8,128)}, ...) | async-done | bytes 7176208 | tf_op jit(solution)/shard_map/psum | solution.py:326
  (353 shorter events, 141.3 us)
Async XLA Ops:
  7.2 422.3 %copy-start = (bf16[768,768]{1,0:T(8,128)(2,1)S(1)}, bf16[768,768]{1,0:T(8,128)(2,1)}, u32[]{:S(2)}) copy-start(bf16[768,768]{1,0:T(8,128)(2,1)} %param.34) | copy-start | bytes 3538948
  7.2 72.0 %all-gather.11.cloned.1.call-start = ((), (), s32[]{:S(2)}) async-start(), calls=%async_computation.4 | async-start | bytes 3932160 | tf_op jit(solution)/shard_map/all_gather | solution.py:95
  8.8 4.9 copy-start.75
  8.8 70.4 %copy-start.98 = (bf16[768,3,192]{0,2,1:T(8,128)(2,1)S(1)}, bf16[768,3,192]{0,2,1:T(8,128)(2,1)}, u32[]{:S(2)}) copy-start(bf16[768,3,192]{0,2,1:T(8,128)(2,1)} %param.24) | copy-start | bytes 2654212
  12.8 285.1 %reduce-scatter.5.cloned.1.call-start = ((), (), s32[]{:S(2)}) async-start(), calls=%async_computation.5 | async-start | bytes 7864320 | tf_op jit(solution)/shard_map/reduce_scatter | solution.py:160
  83.1 6.6 copy-start.34
  87.5 22.8 %copy-start.5 = (f32[2048,3,64]{0,2,1:T(8,128)}, f32[2048,3,64]{0,2,1:T(8,128)S(1)}, u32[]{:S(2)}) copy-start(f32[2048,3,64]{0,2,1:T(8,128)S(1)} %get-tuple-element.454) | copy-start | bytes 4718596
  117.1 10.1 %copy-start.11 = (f32[2048,3,64]{0,2,1:T(8,128)S(1)}, f32[2048,3,64]{0,2,1:T(8,128)}, u32[]{:S(2)}) copy-start(f32[2048,3,64]{0,2,1:T(8,128)} %get-tuple-element.448) | copy-start | bytes 4718596
  117.1 10.1 %copy-start.48 = (f32[2048,3]{0,1:T(4,128)S(1)}, f32[2048,3]{0,1:T(4,128)}, u32[]{:S(2)}) copy-start(f32[2048,3]{0,1:T(4,128)} %get-tuple-element.447) | copy-start | bytes 73732
  121.4 5.8 copy-start.59
  161.7 7.7 copy-start.71
  161.7 5.7 copy-start.36
  161.7 5.7 copy-start.37
  169.3 7.3 copy-start.57
  169.4 7.3 copy-start.100
  171.9 4.7 copy-start.61
  171.9 4.8 copy-start.20
  188.3 177.6 %all-gather.13.cloned.1.call-start = ((), (), s32[]{:S(2)}) async-start(), calls=%async_computation.6 | async-start | bytes 3932160 | tf_op jit(solution)/shard_map/all_gather | solution.py:171
  301.7 127.8 %all-gather.15.cloned.1.call-start = ((), (), s32[]{:S(2)}) async-start(), calls=%async_computation.8 | async-start | bytes 3932160 | tf_op jit(solution)/shard_map/all_gather | solution.py:185
  302.3 255.3 %reduce-scatter.9.cloned.1.call-start = ((), (), s32[]{:S(2)}) async-start(), calls=%async_computation.9 | async-start | bytes 7864320 | tf_op jit(solution)/shard_map/reduce_scatter | solution.py:198
  429.5 13.9 %copy-start.97 = (bf16[768,768]{1,0:T(8,128)(2,1)S(1)}, bf16[768,768]{1,0:T(8,128)(2,1)}, u32[]{:S(2)}) copy-start(bf16[768,768]{1,0:T(8,128)(2,1)} %param.32) | copy-start | bytes 3538948
  448.0 172.5 %reduce-scatter.7.cloned.1.call-start = ((), (), s32[]{:S(2)}) async-start(), calls=%async_computation.7 | async-start | bytes 3932160 | tf_op jit(solution)/shard_map/reduce_scatter | solution.py:177
  454.4 235.5 %all-gather.17.cloned.1.call-start = ((), (), s32[]{:S(2)}) async-start(), calls=%async_computation.10 | async-start | bytes 3932160 | tf_op jit(solution)/shard_map/all_gather | solution.py:207
  455.0 105.2 %copy-start.79 = (f32[512]{0:T(512)S(1)}, f32[512]{0:T(512)}, u32[]{:S(2)}) copy-start(f32[512]{0:T(512)} %copy-done.78) | copy-start | bytes 6148
  560.2 64.8 %copy-start.32 = (bf16[512,768]{1,0:T(8,128)(2,1)S(1)}, bf16[512,768]{1,0:T(8,128)(2,1)}, u32[]{:S(2)}) copy-start(bf16[512,768]{1,0:T(8,128)(2,1)} %param.37) | copy-start | bytes 2359300
  625.0 64.9 %copy-start.53 = (bf16[192,768]{1,0:T(8,128)(2,1)S(1)}, bf16[192,768]{1,0:T(8,128)(2,1)}, u32[]{:S(2)}) copy-start(bf16[192,768]{1,0:T(8,128)(2,1)} %param.28) | copy-start | bytes 884740
  626.2 243.1 %reduce-scatter.11.cloned.1.call-start = ((), (), s32[]{:S(2)}) async-start(), calls=%async_computation.11 | async-start | bytes 3932160 | tf_op jit(solution)/shard_map/reduce_scatter | solution.py:312
  692.9 7.9 copy-start.58
  693.0 7.9 copy-start.62
  695.6 5.3 copy-start.56
  695.6 5.4 copy-start.24
  695.6 5.4 copy-start.27
  701.0 10.8 %copy-start.23 = (bf16[32,64,3,128]{3,1,2,0:T(8,128)(2,1)S(1)}, bf16[32,64,3,128]{3,1,2,0:T(8,128)(2,1)}, u32[]{:S(2)}) copy-start(bf16[32,64,3,128]{3,1,2,0:T(8,128)(2,1)} %copy-done.22) | copy-start | bytes 4718596
  716.1 9.5 copy-start.28
  725.7 7.3 copy-start.87
  733.0 5.7 copy-start.13
  738.7 4.8 copy-start.21
  743.5 4.5 copy-start.25
  797.4 4.9 copy-start.51
  810.2 181.0 %all-reduce.5.cloned.1.call-start = ((), (), s32[]{:S(2)}) async-start(), calls=%async_computation.12 | async-start | bytes 14548992 | tf_op jit(solution)/shard_map/psum | solution.py:326
  810.5 7.1 copy-start.96
  810.5 7.1 copy-start.103
  817.5 7.2 copy-start.38
  829.8 39.5 %copy-start.68 = (f32[768]{0:T(1024)S(1)}, f32[768]{0:T(1024)}, u32[]{:S(2)}) copy-start(f32[768]{0:T(1024)} %copy-done.67) | copy-start | bytes 9220
  829.8 39.5 %copy-start.70 = (f32[512]{0:T(512)S(1)}, f32[512]{0:T(512)}, u32[]{:S(2)}) copy-start(f32[512]{0:T(512)} %copy-done.69) | copy-start | bytes 6148
  829.9 41.3 %copy-start.77 = (f32[512]{0:T(512)S(1)}, f32[512]{0:T(512)}, u32[]{:S(2)}) copy-start(f32[512]{0:T(512)} %copy-done.76) | copy-start | bytes 6148
  829.9 41.3 %copy-start.74 = (f32[512]{0:T(512)S(1)}, f32[512]{0:T(512)}, u32[]{:S(2)}) copy-start(f32[512]{0:T(512)} %copy-done.73) | copy-start | bytes 6148
  830.0 43.3 %copy-start.19 = (f32[512,768]{1,0:T(8,128)S(1)}, f32[512,768]{1,0:T(8,128)}, u32[]{:S(2)}) copy-start(f32[512,768]{1,0:T(8,128)} %copy-done.18) | copy-start | bytes 4718596
  (65 other events, 172.5 us)
Sparse Core Ops, SparseCore 0:
  12.9 66.1 all-gather.10
  188.4 109.4 reduce-scatter.4
  301.8 64.0 all-gather.12
  367.3 62.1 all-gather.14
  448.2 109.3 reduce-scatter.8
  559.8 60.7 reduce-scatter.6
  626.3 63.5 all-gather.16
  810.4 58.9 reduce-scatter.10
  874.4 116.7 all-reduce.4
where the time goes:
time: 1020 us; the launch traced here: 1010 us
  waiting for transfers between devices  625 us (61%)
  matrix products  136 us (13%)
  local copies, waits for them, and re-layouts  86.1 us (8%)
  other arithmetic  72.6 us (7%)
  blocking collectives  69.3 us (7%)
  between operations  15.4 us (2%)
    reduce_scatter x1, waiting for transfers between devices, shards(): lax.psum_scatter(jnp.dot(attended_low, output_weight, preferred_element_t...  108 us
    reduce_scatter x1, waiting for transfers between devices, shards(): lax.psum_scatter(jnp.einsum('tf,df->td', hidden_low, inner_weight, prefer...  103 us
    psum x1, waiting for transfers between devices, shards(): lax.psum((mixer_delta, mixer_bias_delta, feature_weight_delta, feature_bi...  70.3 us
    all_gather x1, waiting for transfers between devices, shards(): first_rows = lax.all_gather(first_low, 'tp', axis=0, tiled=True)  65 us
    all_gather x1, waiting for transfers between devices, shards(): second_rows = lax.all_gather(second_low, 'tp', axis=0, tiled=True)  62.3 us
    all_gather x1, waiting for transfers between devices, shards(): middle_rows = lax.all_gather(middle_low, 'tp', axis=0, tiled=True)  60.4 us
    reduce_scatter x1, waiting for transfers between devices, shards(): lax.psum_scatter(jnp.dot(activated, outer_weight, preferred_element_type=...  60.3 us
    all_gather x1, waiting for transfers between devices, shards(): upstream_rows = lax.all_gather(cotangent, 'tp', axis=0, tiled=True)  56.1 us
  transfers between devices with their start and end apart: 9, of which 9 were waited for; matrix products, arithmetic and copies ran while one was open for 5% of the time, Pallas kernels for 0%

commit v1 on v0

--- a/solution.py
+++ b/solution.py
@@ -168,7 +168,9 @@
         layer_norm, middle, second_gain.astype(jnp.float32), second_bias.astype(jnp.float32)
     )
     second_low = second_normed.astype(jnp.bfloat16)
-    second_rows = lax.all_gather(second_low, "tp", axis=0, tiled=True)
+    second_rows = jnp.concatenate(
+        lax.all_to_all(jnp.stack([second_low] * lax.axis_size("tp")), "tp", 0, 0), axis=0
+    )
     hidden_input = jnp.dot(
         second_rows, inner_weight, preferred_element_type=jnp.float32
     ) + inner_bias.astype(jnp.float32)

time: 1020 us -> 1020 us (level)
    all_to_all x0 -> x1, waiting for transfers between devices: none -> 120 us  [shards(): lax.all_to_all(jnp.stack([second_low] * lax.axis_size('tp')), 'tp', 0, 0)]
    all_gather x1 -> x0, waiting for transfers between devices: 62.3 us -> none  [shards(): second_rows = lax.all_gather(second_low, 'tp', axis=0, tiled=True)]
    all_gather x1, waiting for transfers between devices: 56.1 us -> 0.01 us  [shards(): upstream_rows = lax.all_gather(cotangent, 'tp', axis=0, tiled=True)]
  transfers between devices with their start and end apart: 9 -> 9, of which waited for: 9 -> 8; matrix products, arithmetic and copies ran while one was open for 5% -> 5% of each run, Pallas kernels for 0% -> 0%
where the time goes in v1:
time: 1020 us; the launch traced here: 1010 us
  waiting for transfers between devices  626 us (61%)
  matrix products  136 us (13%)
  local copies, waits for them, and re-layouts  87.9 us (9%)
  other arithmetic  71.7 us (7%)
  blocking collectives  69.3 us (7%)
  between operations  15.7 us (2%)
    all_to_all x1, waiting for transfers between devices, shards(): lax.all_to_all(jnp.stack([second_low] * lax.axis_size('tp')), 'tp', 0, 0)  120 us
    reduce_scatter x1, waiting for transfers between devices, shards(): lax.psum_scatter(jnp.dot(attended_low, output_weight, preferred_element_t...  108 us
    reduce_scatter x1, waiting for transfers between devices, shards(): lax.psum_scatter(jnp.einsum('tf,df->td', hidden_low, inner_weight, prefer...  102 us
    psum x1, waiting for transfers between devices, shards(): lax.psum((mixer_delta, mixer_bias_delta, feature_weight_delta, feature_bi...  70.3 us
    all_gather x1, waiting for transfers between devices, shards(): first_rows = lax.all_gather(first_low, 'tp', axis=0, tiled=True)  65 us
    all_gather x1, waiting for transfers between devices, shards(): middle_rows = lax.all_gather(middle_low, 'tp', axis=0, tiled=True)  60.5 us
    reduce_scatter x1, waiting for transfers between devices, shards(): lax.psum_scatter(jnp.dot(activated, outer_weight, preferred_element_type=...  60.3 us
    reduce_scatter x1, waiting for transfers between devices, shards(): lax.psum_scatter(jnp.einsum('tk,dk->td', mixed_delta, mixer_flat, preferr...  39.3 us
  transfers between devices with their start and end apart: 9, of which 8 were waited for; matrix products, arithmetic and copies ran while one was open for 5% of the time, Pallas kernels for 0%

profile of v1, /device:TPU:0, one launch (start us, length us, event | category | flops | bytes accessed | tf_op | source)
XLA Modules:
  0.0 1013.2 jit_solution(3089321646345442224)
XLA Ops:
  14.2 65.0 %all-gather.10.cloned.1.call-done = bf16[2048,768]{1,0:T(8,128)(2,1)} async-done(((bf16[512,768]{1,0:T(8,128)(2,1)}), bf16[2048,768]{1,0:T(8,128)(2,1)}) %all-gather.10.cloned.1.call-update) | async-done | bytes 3145744 | tf_op jit(solution)/shard_map/all_gather | solution.py:95
  79.2 3.9 add_convert_fusion
  94.3 3.4 reshape_squeeze.3
  97.7 3.4 copy.124
  103.5 3.4 concatenate.19
  106.9 3.4 copy.107
  117.1 4.3 convert_reduce_fusion.3
  121.5 5.6 all-gather.4
  129.8 3.5 copy.115
  135.1 3.4 concatenate.21
  138.5 3.5 copy.114
  147.0 7.0 all-gather
  154.0 6.5 while.34
  161.7 5.7 multiply_add_fusion.3
  171.9 4.7 fusion.25
  184.6 3.7 fusion.127
  189.5 108.3 %reduce-scatter.5.cloned.1.call-done = f32[512,768]{1,0:T(8,128)} async-done(((f32[2048,768]{1,0:T(8,128)}), f32[512,768]{1,0:T(8,128)}) %reduce-scatter.5.cloned.1.call-update) | async-done | bytes 1572880 | tf_op jit(solution)/shard_map/reduce_scatter | solution.py:160
  302.6 4.7 all-to-all-start
  309.4 119.8 %all-to-all-done = bf16[4,512,768]{2,1,0:T(8,128)(2,1)} async-done(((bf16[4,512,768]{2,1,0:T(8,128)(2,1)}), bf16[4,512,768]{2,1,0:T(8,128)(2,1)}, u32[]{:S(2)}, u32[]{:S(2)}) %all-to-all-start) | async-done | bytes 3145760 | tf_op jit(solution)/shard_map/all_to_all | solution.py:172
  429.2 7.5 fusion.128
  436.7 12.2 %convert_reduce_fusion = (f32[768]{0:T(1024)}, bf16[2048,768]{1,0:T(8,128)(2,1)S(1)}, bf16[2048,768]{1,0:T(8,128)(2,1)}) fusion(f32[2048,768]{1,0:T(8,128)} %fusion.128, f32[768]{0:T(1024)} %convert_element_type.136, bf16[2048,768]{1,0:T(8,128)(2,1)} %all-gather.12.cloned.1.call-done, bf16[768,768]{1,0:T(8,128)(2,1)S(1)} %copy-done), kind=kOutput, calls=%fused_computation.18 | convolution fusion | flops 2461531392 | bytes 16914432 | tf_op jit(solution)/shard_map/td,fd->tf/dot_general | solution.py:191
  450.6 4.6 fusion.129
  455.3 6.2 convolution_convert_fusion
  462.1 102.1 %reduce-scatter.9.cloned.1.call-done = f32[512,768]{1,0:T(8,128)} async-done(((f32[2048,768]{1,0:T(8,128)}), f32[512,768]{1,0:T(8,128)}) %reduce-scatter.9.cloned.1.call-update) | async-done | bytes 1572880 | tf_op jit(solution)/shard_map/reduce_scatter | solution.py:200
  566.9 60.3 %reduce-scatter.7.cloned.1.call-done = bf16[512,768]{1,0:T(8,128)(2,1)} async-done(((bf16[2048,768]{1,0:T(8,128)(2,1)}), bf16[512,768]{1,0:T(8,128)(2,1)}) %reduce-scatter.7.cloned.1.call-update) | async-done | bytes 786448 | tf_op jit(solution)/shard_map/reduce_scatter | solution.py:179
  636.1 60.5 %all-gather.14.cloned.1.call-done = bf16[2048,768]{1,0:T(8,128)(2,1)} async-done(((bf16[512,768]{1,0:T(8,128)(2,1)}), bf16[2048,768]{1,0:T(8,128)(2,1)}) %all-gather.14.cloned.1.call-update) | async-done | bytes 3145744 | tf_op jit(solution)/shard_map/all_gather | solution.py:209
  702.2 5.2 multiply_reduce_fusion
  707.6 10.8 %fusion.23 = f32[32,3,128,64]{2,3,1,0:T(8,128)} fusion(f32[32,3,64,128]{3,0,2,1:T(8,128)S(1)} %copy-done.27, f32[32,64,3,64]{1,0,3,2:T(8,128)S(1)} %copy-done.24, f32[32,64,3]{1,2,0:T(4,128)S(1)} %copy-done.56), kind=kOutput, calls=%fused_computation.50 | convolution fusion | flops 604372992 | bytes 7888896 | tf_op jit(solution)/shard_map/jthe,jhef->jthf/dot_general | solution.py:239
  718.4 4.3 fusion.111
  724.2 5.2 all-gather.5
  732.3 6.5 all-gather.2
  739.6 5.7 multiply_add_fusion.2
  745.3 4.8 fusion.15
  750.2 4.5 fusion.17
  754.7 4.4 select_convert_fusion
  763.1 4.9 bitcast_add_fusion
  773.9 3.7 fusion.119
  782.7 3.4 copy.181
  788.4 3.6 fusion.118
  797.5 3.6 copy.179
  804.0 4.9 fusion.113
  812.7 4.1 convolution_convert_fusion.1
  817.0 7.0 fusion.131
  824.1 4.1 fusion.132
  836.5 39.3 %reduce-scatter.11.cloned.1.call-done = bf16[512,768]{1,0:T(8,128)(2,1)} async-done(((bf16[2048,768]{1,0:T(8,128)(2,1)}), bf16[512,768]{1,0:T(8,128)(2,1)}) %reduce-scatter.11.cloned.1.call-update) | async-done | bytes 786448 | tf_op jit(solution)/shard_map/reduce_scatter | solution.py:314
  881.9 26.5 %all-reduce = (f32[768]{0:T(1024)S(1)}, f32[768]{0:T(1024)S(1)}, f32[3,192]{1,0:T(4,128)}, f32[2,3,64]{2,1,0:T(4,128)S(1)}, f32[768]{0:T(1024)S(1)}, /*index=5*/...) all-reduce(f32[768]{0:T(1024)S(1)} %get-tuple-element.373, ...), channel_id=1, replica_groups=mesh['dp'=2,'ctx'=4,'tp'=4] {'dp','ctx'}, use_global_device_ids=true, to_apply=%region_32.33 | all-reduce | flops 6336 | bytes 50688 | tf_op jit(solution)/shard_map/psum | solution.py:328
  909.0 18.5 %all-reduce.2 = (f32[768]{0:T(1024)}, f32[768]{0:T(1024)}, f32[768]{0:T(1024)}, f32[768]{0:T(1024)}, f32[768]{0:T(1024)}, /*index=5*/f32[768]{0:T(1024)}) all-reduce(f32[768]{0:T(1024)S(1)} %get-tuple-element.404, f32[768]{0:T(1024)S(1)} %get-tuple-element.405, ...), channel_id=1, replica_groups=mesh['dp'=2,'ctx'=4,'tp'=4] {'tp'}, use_global_device_ids=true, to_apply=%region_33.34 | all-reduce | flops 4608 | bytes 36864 | tf_op jit(solution)/shard_map/psum | solution.py:347
  927.5 70.3 %all-reduce.5.cloned.1.call-done = (f32[768,3,192]{0,2,1:T(8,128)}, f32[2,3,64,64]{3,2,1,0:T(8,128)}, f32[192,768]{1,0:T(8,128)}, f32[768,768]{1,0:T(8,128)}, f32[768,768]{1,0:T(8,128)}) async-done(((f32[768,3,192]{0,2,1:T(8,128)}, f32[2,3,64,64]{3,2,1,0:T(8,128)}, f32[192,768]{1,0:T(8,128)}, f32[768,768]{1,0:T(8,128)}, f32[768,768]{1,0:T(8,128)}), (f32[768,3,192]{0,2,1:T(8,128)}, ...) | async-done | bytes 7176208 | tf_op jit(solution)/shard_map/psum | solution.py:328
  (353 shorter events, 142.3 us)
Async XLA Ops:
  7.2 429.5 %copy-start = (bf16[768,768]{1,0:T(8,128)(2,1)S(1)}, bf16[768,768]{1,0:T(8,128)(2,1)}, u32[]{:S(2)}) copy-start(bf16[768,768]{1,0:T(8,128)(2,1)} %param.34) | copy-start | bytes 3538948
  7.2 72.0 %all-gather.10.cloned.1.call-start = ((), (), s32[]{:S(2)}) async-start(), calls=%async_computation.5 | async-start | bytes 3932160 | tf_op jit(solution)/shard_map/all_gather | solution.py:95
  8.8 4.9 copy-start.75
  8.8 70.4 %copy-start.98 = (bf16[768,3,192]{0,2,1:T(8,128)(2,1)S(1)}, bf16[768,3,192]{0,2,1:T(8,128)(2,1)}, u32[]{:S(2)}) copy-start(bf16[768,3,192]{0,2,1:T(8,128)(2,1)} %param.24) | copy-start | bytes 2654212
  12.8 285.0 %reduce-scatter.5.cloned.1.call-start = ((), (), s32[]{:S(2)}) async-start(), calls=%async_computation.6 | async-start | bytes 7864320 | tf_op jit(solution)/shard_map/reduce_scatter | solution.py:160
  83.1 6.6 copy-start.34
  87.4 22.8 %copy-start.5 = (f32[2048,3,64]{0,2,1:T(8,128)}, f32[2048,3,64]{0,2,1:T(8,128)S(1)}, u32[]{:S(2)}) copy-start(f32[2048,3,64]{0,2,1:T(8,128)S(1)} %get-tuple-element.454) | copy-start | bytes 4718596
  117.1 10.1 copy-start.11
  117.1 10.1 copy-start.48
  121.4 5.8 copy-start.59
  161.6 7.7 copy-start.71
  161.6 5.7 copy-start.36
  161.7 5.7 copy-start.37
  169.3 7.3 copy-start.57
  169.3 7.3 copy-start.100
  171.9 4.7 copy-start.61
  171.9 4.8 copy-start.20
  302.6 126.6 %all-to-all-start = ((bf16[4,512,768]{2,1,0:T(8,128)(2,1)}), bf16[4,512,768]{2,1,0:T(8,128)(2,1)}, u32[]{:S(2)}, u32[]{:S(2)}) async-start(bf16[4,512,768]{2,1,0:T(8,128)(2,1)} %stack.30), calls=%async_computation.1 | async-start | bytes 6291456 | tf_op jit(solution)/shard_map/all_to_all | solution.py:172
  307.3 129.4 %all-gather.12.cloned.1.call-start = ((), (), s32[]{:S(2)}) async-start(), calls=%async_computation.8 | async-start | bytes 3932160 | tf_op jit(solution)/shard_map/all_gather | solution.py:187
  308.0 256.2 %reduce-scatter.9.cloned.1.call-start = ((), (), s32[]{:S(2)}) async-start(), calls=%async_computation.9 | async-start | bytes 7864320 | tf_op jit(solution)/shard_map/reduce_scatter | solution.py:200
  436.7 14.0 %copy-start.97 = (bf16[768,768]{1,0:T(8,128)(2,1)S(1)}, bf16[768,768]{1,0:T(8,128)(2,1)}, u32[]{:S(2)}) copy-start(bf16[768,768]{1,0:T(8,128)(2,1)} %param.32) | copy-start | bytes 3538948
  455.2 172.0 %reduce-scatter.7.cloned.1.call-start = ((), (), s32[]{:S(2)}) async-start(), calls=%async_computation.7 | async-start | bytes 3932160 | tf_op jit(solution)/shard_map/reduce_scatter | solution.py:179
  461.5 235.1 %all-gather.14.cloned.1.call-start = ((), (), s32[]{:S(2)}) async-start(), calls=%async_computation.10 | async-start | bytes 3932160 | tf_op jit(solution)/shard_map/all_gather | solution.py:209
  462.1 104.7 %copy-start.79 = (f32[512]{0:T(512)S(1)}, f32[512]{0:T(512)}, u32[]{:S(2)}) copy-start(f32[512]{0:T(512)} %copy-done.78) | copy-start | bytes 6148
  566.9 64.7 %copy-start.32 = (bf16[512,768]{1,0:T(8,128)(2,1)S(1)}, bf16[512,768]{1,0:T(8,128)(2,1)}, u32[]{:S(2)}) copy-start(bf16[512,768]{1,0:T(8,128)(2,1)} %param.37) | copy-start | bytes 2359300
  631.6 64.9 %copy-start.53 = (bf16[192,768]{1,0:T(8,128)(2,1)S(1)}, bf16[192,768]{1,0:T(8,128)(2,1)}, u32[]{:S(2)}) copy-start(bf16[192,768]{1,0:T(8,128)(2,1)} %param.28) | copy-start | bytes 884740
  632.8 243.1 %reduce-scatter.11.cloned.1.call-start = ((), (), s32[]{:S(2)}) async-start(), calls=%async_computation.11 | async-start | bytes 3932160 | tf_op jit(solution)/shard_map/reduce_scatter | solution.py:314
  699.6 7.9 copy-start.58
  699.6 7.9 copy-start.62
  702.2 5.3 copy-start.56
  702.2 5.4 copy-start.24
  702.2 5.4 copy-start.27
  707.6 10.8 %copy-start.23 = (bf16[32,64,3,128]{3,1,2,0:T(8,128)(2,1)S(1)}, bf16[32,64,3,128]{3,1,2,0:T(8,128)(2,1)}, u32[]{:S(2)}) copy-start(bf16[32,64,3,128]{3,1,2,0:T(8,128)(2,1)} %copy-done.22) | copy-start | bytes 4718596
  722.8 9.5 copy-start.28
  732.3 7.3 copy-start.87
  739.6 5.7 copy-start.13
  745.3 4.8 copy-start.21
  750.2 4.5 copy-start.25
  804.0 4.9 copy-start.51
  816.8 181.0 %all-reduce.5.cloned.1.call-start = ((), (), s32[]{:S(2)}) async-start(), calls=%async_computation.12 | async-start | bytes 14548992 | tf_op jit(solution)/shard_map/psum | solution.py:328
  817.0 7.1 copy-start.96
  817.0 7.1 copy-start.102
  824.1 7.2 copy-start.38
  836.4 39.5 %copy-start.68 = (f32[768]{0:T(1024)S(1)}, f32[768]{0:T(1024)}, u32[]{:S(2)}) copy-start(f32[768]{0:T(1024)} %copy-done.67) | copy-start | bytes 9220
  836.4 39.5 %copy-start.70 = (f32[512]{0:T(512)S(1)}, f32[512]{0:T(512)}, u32[]{:S(2)}) copy-start(f32[512]{0:T(512)} %copy-done.69) | copy-start | bytes 6148
  836.4 41.3 %copy-start.77 = (f32[512]{0:T(512)S(1)}, f32[512]{0:T(512)}, u32[]{:S(2)}) copy-start(f32[512]{0:T(512)} %copy-done.76) | copy-start | bytes 6148
  836.4 41.3 %copy-start.74 = (f32[512]{0:T(512)S(1)}, f32[512]{0:T(512)}, u32[]{:S(2)}) copy-start(f32[512]{0:T(512)} %copy-done.73) | copy-start | bytes 6148
  836.5 43.3 %copy-start.19 = (f32[512,768]{1,0:T(8,128)S(1)}, f32[512,768]{1,0:T(8,128)}, u32[]{:S(2)}) copy-start(f32[512,768]{1,0:T(8,128)} %copy-done.18) | copy-start | bytes 4718596
  (65 other events, 172.3 us)
Sparse Core Ops, SparseCore 0:
  12.9 66.1 all-gather.9
  188.4 109.4 reduce-scatter.4
  309.7 111.9 all-gather.11
  455.3 108.8 reduce-scatter.8
  566.4 60.7 reduce-scatter.6
  632.9 63.5 all-gather.13
  816.9 58.9 reduce-scatter.10
  880.9 116.7 all-reduce.4
